TPU v7x, 256 devices: a whole 4x4x8 slice. The times are simulated.
256 devices in a mesh: energy: 32 (over x, y, core), space: 8 (over z).
Axes of the slice: x: 4, y: 4, z: 8, core: 2. Of those that a mesh axis runs over, the one named last changes fastest.
Arguments:
- onsite: float32 [8, 2, 128, 128], P('space'), may hold values from -0.25 to 0.25
- hopping: float32 [8, 2, 128, 128], P('space'), may hold values from -0.25 to 0.25
- sigma_old: float32 [32, 8, 2, 128, 128], P('energy', 'space'), may hold values from -0.0390625 to 0.0390625
- screened: float32 [32, 8, 2, 3, 2, 128, 128], P('energy', 'space'), may hold values from -1 to 1
Outputs:
- green_retarded: float32 [32, 8, 3, 2, 128, 128], P('energy', 'space')
- self_energy: float32 [32, 8, 2, 3, 2, 128, 128], P('energy', 'space')
All inputs are finite; a program needn't handle non-finite values.
Results may differ from a plain program's by a relative error of at most 0.0003.
Values sent between devices are 32-bit elements; how exact they have to be, the bound alone decides.
A program may use at most 128 MiB of HBM per device.

v0:
```python
import math
import jax
import jax.numpy as jnp
from jax import lax
from jax.sharding import PartitionSpec as P

BROADEN = 0.45
THERMAL = 0.1
PRECISE = lax.Precision.HIGHEST


def passed_along(block, axis, distance):
    devices = range(lax.axis_size(axis))
    route = [(i - distance, i) for i in devices if i - distance in devices]
    return lax.ppermute(block, axis, route)


def matmul_high(first, second):
    return jnp.matmul(first, second, precision=PRECISE)


def complex_product(first, second):
    real_part = matmul_high(first[0], second[0]) - matmul_high(first[1], second[1])
    imag_part = matmul_high(first[0], second[1]) + matmul_high(first[1], second[0])
    return jnp.stack([real_part, imag_part])


def dagger(blocks):
    return jnp.stack([jnp.swapaxes(blocks[0], -1, -2), -jnp.swapaxes(blocks[1], -1, -2)])


def invert(blocks):
    size_order = blocks.shape[-1]
    normal_complex = complex_product(dagger(blocks), blocks)
    upper_normal = jnp.concatenate([normal_complex[0], -normal_complex[1]], axis=-1)
    lower_normal = jnp.concatenate([normal_complex[1], normal_complex[0]], axis=-1)
    normal = jnp.concatenate([upper_normal, lower_normal], axis=-2)
    factor = jnp.linalg.cholesky(normal)
    right_side = jnp.concatenate(
        [jnp.swapaxes(blocks[0], -1, -2), -jnp.swapaxes(blocks[1], -1, -2)], axis=-2
    )
    middle = lax.linalg.triangular_solve(factor, right_side, left_side=True, lower=True)
    solved = lax.linalg.triangular_solve(
        factor, middle, left_side=True, lower=True, transpose_a=True
    )
    return jnp.stack([solved[..., :size_order, :], solved[..., size_order:, :]])


def spectrum_forward(cosines, sines, values):
    energies_all = values.shape[0]
    real_part = values[:, :, :, 0].reshape(energies_all, -1)
    imag_part = values[:, :, :, 1].reshape(energies_all, -1)
    return (
        matmul_high(cosines, real_part) + matmul_high(sines, imag_part),
        matmul_high(cosines, imag_part) - matmul_high(sines, real_part),
    )


def paired_inverse(system_pair, outer_pair, carried, inner_pair):
    return invert(system_pair - complex_product(outer_pair, complex_product(carried, inner_pair)))


def local(onsite, hopping, sigma_old, screened):
    local_count = sigma_old.shape[0]
    size_order = sigma_old.shape[-1]
    groups = lax.axis_size("energy")
    energies_all = local_count * groups
    segments = lax.axis_size("space")
    position = lax.axis_index("space")
    is_first = position == 0
    indices = (lax.axis_index("energy") * local_count + jnp.arange(local_count)).astype(jnp.float32)
    energy = -1.5 + 3.0 * (indices + 0.5) / energies_all
    identity = jnp.eye(size_order, dtype=jnp.float32)
    hamiltonian = 0.5 * (onsite[0] + dagger(onsite[0]))
    coupling = hopping[0]
    local_sigma = jnp.moveaxis(sigma_old[:, 0], 1, 0)
    system = jnp.stack(
        [
            energy[:, None, None] * identity - hamiltonian[0] - local_sigma[0],
            BROADEN * identity - hamiltonian[1] - local_sigma[1],
        ]
    )
    magnitude = energy * energy + BROADEN * BROADEN
    contact_green = jnp.stack(
        [
            (energy / magnitude)[:, None, None] * identity,
            (-BROADEN / magnitude)[:, None, None] * identity,
        ]
    )
    next_coupling = passed_along(coupling, "space", -1)
    system_pair = jnp.stack([system, system], axis=1)
    outer_pair = jnp.stack([dagger(coupling), next_coupling], axis=1)[:, :, None]
    inner_pair = jnp.stack([coupling, dagger(next_coupling)], axis=1)[:, :, None]

    def sweep(iteration, received):
        fresh = paired_inverse(system_pair, outer_pair, received, inner_pair)
        got_left = passed_along(fresh[:, 0], "space", 1)
        got_left = jnp.where(is_first, contact_green, got_left)
        got_right = passed_along(fresh[:, 1], "space", -1)
        return jnp.stack([got_left, got_right], axis=1)

    start_left = jnp.where(is_first, contact_green, jnp.zeros_like(contact_green))
    start_pair = jnp.stack([start_left, jnp.zeros_like(contact_green)], axis=1)
    final_pair = lax.fori_loop(0, segments - 1, sweep, start_pair)
    previous = final_pair[:, 0]
    following = final_pair[:, 1]
    self_left = complex_product(dagger(coupling), complex_product(previous, coupling))
    self_right = complex_product(next_coupling, complex_product(following, dagger(next_coupling)))
    diagonal = invert(system - self_left - self_right)
    upper_block = complex_product(previous, complex_product(coupling, diagonal))
    lower_block = complex_product(diagonal, complex_product(dagger(coupling), previous))
    stacked = jnp.stack([diagonal, upper_block, lower_block], axis=2)
    green_out = jnp.transpose(stacked, (1, 2, 0, 3, 4))[:, None]
    spectral = jnp.stack(
        [
            diagonal - dagger(diagonal),
            upper_block - dagger(lower_block),
            lower_block - dagger(upper_block),
        ],
        axis=2,
    )
    kernels = screened.reshape(local_count, 2, 3, 2, size_order * size_order)
    occupation = 1.0 / (1.0 + jnp.exp(energy / THERMAL))
    occupied = occupation[None, :, None, None, None]
    both_kinds = jnp.stack([-occupied * spectral, (1.0 - occupied) * spectral])
    outgoing = jnp.transpose(both_kinds, (2, 0, 3, 1, 4, 5)).reshape(
        local_count, 2, 3, 2, size_order * size_order
    )
    gathered, spectra = (
        lax.all_to_all(outgoing, "energy", split_axis=4, concat_axis=0, tiled=True),
        lax.all_to_all(kernels, "energy", split_axis=4, concat_axis=0, tiled=True),
    )
    padded_length = 2 * energies_all
    frequency = jnp.arange(padded_length, dtype=jnp.int32)[:, None]
    position_grid = jnp.arange(energies_all, dtype=jnp.int32)[None, :]
    phases = (frequency * position_grid % padded_length).astype(jnp.float32) * (
        2.0 * math.pi / padded_length
    )
    cosines = jnp.cos(phases)
    sines = jnp.sin(phases)
    green_real, green_imag = spectrum_forward(cosines, sines, gathered)
    kernel_real, kernel_imag = spectrum_forward(cosines, sines, spectra)
    product_real = green_real * kernel_real - green_imag * kernel_imag
    product_imag = green_real * kernel_imag + green_imag * kernel_real
    back_cosines = jnp.transpose(cosines) / padded_length
    back_sines = jnp.transpose(sines) / padded_length
    conv_real = matmul_high(back_cosines, product_real) - matmul_high(back_sines, product_imag)
    conv_imag = matmul_high(back_cosines, product_imag) + matmul_high(back_sines, product_real)
    slice_width = gathered.shape[-1]
    conv_real = conv_real.reshape(energies_all, 2, 3, slice_width)
    conv_imag = conv_imag.reshape(energies_all, 2, 3, slice_width)
    sigma_elements = jnp.stack([-conv_imag, conv_real], axis=3)
    sigma_local = lax.all_to_all(sigma_elements, "energy", split_axis=0, concat_axis=4, tiled=True)
    sigma_out = sigma_local.reshape(local_count, 1, 2, 3, 2, size_order, size_order)
    return (green_out, sigma_out)


def solution(mesh):
    placed = (
        P("space", None, None, None),
        P("space", None, None, None),
        P("energy", "space", None, None, None),
        P("energy", "space", None, None, None, None, None),
    )
    return jax.shard_map(
        local,
        mesh=mesh,
        in_specs=placed,
        out_specs=(
            P("energy", "space", None, None, None, None),
            P("energy", "space", None, None, None, None, None),
        ),
        check_vma=False,
    )
```

profile of v0, /device:TPU:1, one launch (start us, length us, event | category | flops | bytes accessed | tf_op | source)
XLA Modules:
  0.0 1384.2 jit_solution(7943360227580603645)
XLA Ops:
  3.1 24.3 %copy.351 = f32[1,1,2,3,2,128,128]{3,4,2,6,5,1,0:T(2,128)} copy(f32[1,1,2,3,2,128,128]{6,5,4,3,2,1,0:T(8,128)} %param.9) | data formatting | bytes 1572864 | tf_op args[3]
  27.5 50.3 %reshape.1289 = f32[32,1,6144]{2,1,0:T(1,128)} reshape(f32[16384,1,2,2,3]{4,3,2,1,0:T(2,128)} %bitcast.664) | data formatting | bytes 1572864
  87.5 894.0 %while.14 = (s32[]{:T(128)}, f32[2,2,1,128,128]{4,3,0,2,1:T(8,128)S(1)}, pred[]{:T(512)}, f32[2,2,1,128,128]{4,3,1,2,0:T(8,128)S(1)}, f32[2,2,1,128,128]{4,3,1,2...) while((s32[]{:T(128)}, ...), condition=%wide.region_5.6_spmd, body=%wide.region_0.5_spmd.sunk | while | flops 1009058304 | bytes 19206544 | solution.py:104
  92.7 23.5 %custom-call.47 = f32[2,1,128,128]{3,2,1,0:T(8,128)S(1)} custom-call(f32[2,1,128,128]{3,2,1,0:T(8,128)S(1)} %cholesky.395), custom_call_target="Cholesky" | custom-call | tf_op jit(solution)/shard_map/while/body/eval_jaxpr/jit(cholesky)/cholesky | solution.py:38
  136.6 23.5 %custom-call.49 = f32[2,1,128,128]{3,2,1,0:T(8,128)S(1)} custom-call(f32[2,1,128,128]{3,2,1,0:T(8,128)S(1)} %fusion.435), custom_call_target="Cholesky" | custom-call | tf_op jit(solution)/shard_map/while/body/eval_jaxpr/jit(cholesky)/cholesky | solution.py:38
  164.5 39.3 %custom-call.51 = f32[2,1,2,128,128]{3,4,2,1,0:T(8,128)S(1)} custom-call(f32[2,1,2,128,128]{4,3,2,1,0:T(8,128)S(1)} %bitcast.691), custom_call_target="InvertDiagBlocksLowerTriangular" | custom-call | tf_op jit(solution)/shard_map/while/body/eval_jaxpr/triangular_solve | solution.py:43
  221.7 23.5 %custom-call.47 = f32[2,1,128,128]{3,2,1,0:T(8,128)S(1)} custom-call(f32[2,1,128,128]{3,2,1,0:T(8,128)S(1)} %cholesky.395), custom_call_target="Cholesky" | custom-call | tf_op jit(solution)/shard_map/while/body/eval_jaxpr/jit(cholesky)/cholesky | solution.py:38
  265.5 23.5 %custom-call.49 = f32[2,1,128,128]{3,2,1,0:T(8,128)S(1)} custom-call(f32[2,1,128,128]{3,2,1,0:T(8,128)S(1)} %fusion.435), custom_call_target="Cholesky" | custom-call | tf_op jit(solution)/shard_map/while/body/eval_jaxpr/jit(cholesky)/cholesky | solution.py:38
  293.4 39.3 %custom-call.51 = f32[2,1,2,128,128]{3,4,2,1,0:T(8,128)S(1)} custom-call(f32[2,1,2,128,128]{4,3,2,1,0:T(8,128)S(1)} %bitcast.691), custom_call_target="InvertDiagBlocksLowerTriangular" | custom-call | tf_op jit(solution)/shard_map/while/body/eval_jaxpr/triangular_solve | solution.py:43
  350.4 23.5 %custom-call.47 = f32[2,1,128,128]{3,2,1,0:T(8,128)S(1)} custom-call(f32[2,1,128,128]{3,2,1,0:T(8,128)S(1)} %cholesky.395), custom_call_target="Cholesky" | custom-call | tf_op jit(solution)/shard_map/while/body/eval_jaxpr/jit(cholesky)/cholesky | solution.py:38
  394.2 23.5 %custom-call.49 = f32[2,1,128,128]{3,2,1,0:T(8,128)S(1)} custom-call(f32[2,1,128,128]{3,2,1,0:T(8,128)S(1)} %fusion.435), custom_call_target="Cholesky" | custom-call | tf_op jit(solution)/shard_map/while/body/eval_jaxpr/jit(cholesky)/cholesky | solution.py:38
  422.1 39.3 %custom-call.51 = f32[2,1,2,128,128]{3,4,2,1,0:T(8,128)S(1)} custom-call(f32[2,1,2,128,128]{4,3,2,1,0:T(8,128)S(1)} %bitcast.691), custom_call_target="InvertDiagBlocksLowerTriangular" | custom-call | tf_op jit(solution)/shard_map/while/body/eval_jaxpr/triangular_solve | solution.py:43
  478.3 23.5 %custom-call.47 = f32[2,1,128,128]{3,2,1,0:T(8,128)S(1)} custom-call(f32[2,1,128,128]{3,2,1,0:T(8,128)S(1)} %cholesky.395), custom_call_target="Cholesky" | custom-call | tf_op jit(solution)/shard_map/while/body/eval_jaxpr/jit(cholesky)/cholesky | solution.py:38
  522.2 23.5 %custom-call.49 = f32[2,1,128,128]{3,2,1,0:T(8,128)S(1)} custom-call(f32[2,1,128,128]{3,2,1,0:T(8,128)S(1)} %fusion.435), custom_call_target="Cholesky" | custom-call | tf_op jit(solution)/shard_map/while/body/eval_jaxpr/jit(cholesky)/cholesky | solution.py:38
  550.1 39.3 %custom-call.51 = f32[2,1,2,128,128]{3,4,2,1,0:T(8,128)S(1)} custom-call(f32[2,1,2,128,128]{4,3,2,1,0:T(8,128)S(1)} %bitcast.691), custom_call_target="InvertDiagBlocksLowerTriangular" | custom-call | tf_op jit(solution)/shard_map/while/body/eval_jaxpr/triangular_solve | solution.py:43
  677.3 39.3 %custom-call.51 = f32[2,1,2,128,128]{3,4,2,1,0:T(8,128)S(1)} custom-call(f32[2,1,2,128,128]{4,3,2,1,0:T(8,128)S(1)} %bitcast.691), custom_call_target="InvertDiagBlocksLowerTriangular" | custom-call | tf_op jit(solution)/shard_map/while/body/eval_jaxpr/triangular_solve | solution.py:43
  804.6 39.3 %custom-call.51 = f32[2,1,2,128,128]{3,4,2,1,0:T(8,128)S(1)} custom-call(f32[2,1,2,128,128]{4,3,2,1,0:T(8,128)S(1)} %bitcast.691), custom_call_target="InvertDiagBlocksLowerTriangular" | custom-call | tf_op jit(solution)/shard_map/while/body/eval_jaxpr/triangular_solve | solution.py:43
  931.1 39.3 %custom-call.51 = f32[2,1,2,128,128]{3,4,2,1,0:T(8,128)S(1)} custom-call(f32[2,1,2,128,128]{4,3,2,1,0:T(8,128)S(1)} %bitcast.691), custom_call_target="InvertDiagBlocksLowerTriangular" | custom-call | tf_op jit(solution)/shard_map/while/body/eval_jaxpr/triangular_solve | solution.py:43
  1055.1 30.3 %copy.347 = f32[1,2,3,2,16384]{2,3,1,0,4:T(2,128)} copy(f32[1,2,3,2,16384]{4,0,3,2,1:T(1,128)S(1)} %bitcast.676) | data formatting | bytes 1572864 | tf_op jit(solution)/shard_map/reshape | solution.py:126
  1085.4 50.3 %reshape.1287 = f32[32,1,6144]{2,1,0:T(1,128)} reshape(f32[16384,1,2,2,3]{4,3,2,1,0:T(2,128)} %bitcast.661) | data formatting | bytes 1572864
  1156.8 64.8 %reshape.1290 = f32[16384,1,2,2,3]{4,3,2,1,0:T(2,128)} reshape(f32[32,6144]{1,0:T(8,128)S(1)} %reduce.36) | data formatting | bytes 1572864
  1221.6 26.7 %copy.380 = f32[1,2,3,2,32,512]{5,4,3,2,1,0:T(8,128)S(1)} copy(f32[1,2,3,2,32,512]{2,3,1,5,4,0:T(2,128)} %bitcast.662) | data formatting | bytes 1572864 | tf_op jit(solution)/shard_map/all_to_all | solution.py:131
  1255.7 65.0 %reshape.1288 = f32[16384,1,2,2,3]{4,3,2,1,0:T(2,128)} reshape(f32[32,6144]{1,0:T(8,128)S(1)} %reduce.37) | data formatting | bytes 1572864
  1320.7 26.9 %copy.379 = f32[1,2,3,2,32,512]{5,4,3,2,1,0:T(8,128)S(1)} copy(f32[1,2,3,2,32,512]{2,3,1,5,4,0:T(2,128)} %bitcast.663) | data formatting | bytes 1572864 | tf_op jit(solution)/shard_map/all_to_all | solution.py:130
  (551 shorter events, 607.9 us)
Async XLA Ops:
  1.6 84.8 %copy-start = (f32[1,2,128,128]{3,2,1,0:T(8,128)S(1)}, f32[1,2,128,128]{3,2,1,0:T(8,128)}, u32[]{:S(2)}) copy-start(f32[1,2,128,128]{3,2,1,0:T(8,128)} %param.7) | copy-start | bytes 393220
  1.6 84.9 %copy-start.9 = (f32[1,2,128,128]{3,2,1,0:T(8,128)S(1)}, f32[1,2,128,128]{3,2,1,0:T(8,128)}, u32[]{:S(2)}) copy-start(f32[1,2,128,128]{3,2,1,0:T(8,128)} %param.6) | copy-start | bytes 393220
  1.7 85.2 %copy-start.11 = (f32[1,1,2,128,128]{4,3,2,1,0:T(8,128)S(1)}, f32[1,1,2,128,128]{4,3,2,1,0:T(8,128)}, u32[]{:S(2)}) copy-start(f32[1,1,2,128,128]{4,3,2,1,0:T(8,128)} %param.8) | copy-start | bytes 393220
  1.7 85.6 %collective-permute-start.2 = (f32[2,128,128]{1,2,0:T(8,128)S(1)}, f32[2,128,128]{1,2,0:T(8,128)S(1)}, u32[]{:S(2)}, u32[]{:S(2)}) collective-permute-start(f32[2,128,128]{1,2,0:T(8,128)S(1)} %bitcast.690), channel_id=1, source_target_pairs={{1,0},{2,1},{3,2},{4,3},{5,4},{6,5},{7,6},{9,8},{10,9},{11,10},{12... | collective-permute-start | bytes 393224 | tf_op jit(solution)/shard_map/ppermute | solution.py:15
  77.7 1057.9 %all-to-all-start.1 = ((f32[32,1,6144]{2,1,0:T(1,128)}), f32[32,1,6144]{2,1,0:T(1,128)}, u32[]{:S(2)}, u32[]{:S(2)}) async-start(f32[32,1,6144]{2,1,0:T(1,128)} %reshape.1289), calls=%async_computation.1 | async-start | bytes 1572864 | tf_op jit(solution)/shard_map/all_to_all | solution.py:131
  205.9 6.8 collective-permute-start.1
  210.1 6.7 collective-permute-start
  334.8 5.5 collective-permute-start.1
  338.4 7.2 collective-permute-start
  463.5 6.2 collective-permute-start.1
  467.8 5.7 collective-permute-start
  591.4 5.5 collective-permute-start.1
  595.0 5.8 collective-permute-start
  718.7 5.6 collective-permute-start.1
  722.4 5.7 collective-permute-start
  846.0 4.7 collective-permute-start.1
  848.8 5.7 collective-permute-start
  972.4 5.1 collective-permute-start.1
  975.6 5.7 collective-permute-start
  1135.7 117.5 %all-to-all-start = ((f32[32,1,6144]{2,1,0:T(1,128)}), f32[32,1,6144]{2,1,0:T(1,128)S(1)}, u32[]{:S(2)}, u32[]{:S(2)}) async-start(f32[32,1,6144]{2,1,0:T(1,128)} %reshape.1287), calls=%async_computation | async-start | bytes 1572864 | tf_op jit(solution)/shard_map/all_to_all | solution.py:130
  1320.7 47.9 %copy-start.4 = (f32[128,128]{0,1:T(8,128)S(1)}, f32[128,128]{0,1:T(8,128)}, u32[]{:S(2)}) copy-start(f32[128,128]{0,1:T(8,128)} %copy-done.3) | copy-start | bytes 196612
  1320.7 48.0 %copy-start.6 = (f32[128,128]{0,1:T(8,128)S(1)}, f32[128,128]{0,1:T(8,128)}, u32[]{:S(2)}) copy-start(f32[128,128]{0,1:T(8,128)} %copy-done.5) | copy-start | bytes 196612
  1320.7 48.0 %copy-start.8 = (f32[1,1,128,128]{2,3,0,1:T(8,128)S(1)}, f32[1,1,128,128]{2,3,0,1:T(8,128)}, u32[]{:S(2)}) copy-start(f32[1,1,128,128]{2,3,0,1:T(8,128)} %copy-done.7) | copy-start | bytes 196612
  1361.1 21.6 %all-to-all-start.2 = ((f32[32,2,3,2,512]{4,3,2,1,0:T(2,128)}), f32[32,2,3,2,512]{4,3,2,1,0:T(2,128)S(1)}, u32[]{:S(2)}, u32[]{:S(2)}) async-start(f32[32,2,3,2,512]{4,3,2,1,0:T(2,128)} %copy.355), calls=%async_computation.2 | async-start | bytes 1572864 | tf_op jit(solution)/shard_map/all_to_all | solution.py:153
  (6 other events, 103.0 us)
where the time goes:
time: 1390 us; the launch traced here: 1380 us
  other arithmetic  808 us (58%)
  local copies, waits for them, and re-layouts  384 us (28%)
  matrix products  70.8 us (5%)
  starting transfers between devices  68.7 us (5%)
  waiting for transfers between devices  46.4 us (3%)
    another operation x70, other arithmetic, invert(): factor = jnp.linalg.cholesky(normal)  503 us
    another operation x31, other arithmetic, invert(): lax.linalg.triangular_solve(factor, middle, left_side=True, lower=True, t...  296 us
    unnamed x33, local copies, waits for them, and re-layouts  257 us
    dot_general x132, matrix products, matmul_high(): return jnp.matmul(first, second, precision=PRECISE)  50.5 us
    ppermute x15, starting transfers between devices, passed_along(): return lax.ppermute(block, axis, route)  35.7 us
    ppermute x15, waiting for transfers between devices, passed_along(): return lax.ppermute(block, axis, route)  33.3 us
    another operation x48, local copies, waits for them, and re-layouts  31.5 us
    reshape x1, local copies, waits for them, and re-layouts, local(): jnp.transpose(both_kinds, (2, 0, 3, 1, 4, 5))  30.3 us
  transfers between devices with their start and end apart: 18, of which 15 were waited for; matrix products, arithmetic and copies ran while one was open for 83% of the time, Pallas kernels for 0%

commit v1 on v0

--- a/solution.py
+++ b/solution.py
@@ -61,6 +61,15 @@
 
 
 def local(onsite, hopping, sigma_old, screened):
+
+    def see_fields_on_mesh(local_values):
+        return jnp.concatenate(
+            lax.all_to_all(
+                jnp.stack(jnp.split(local_values, lax.axis_size("energy"), axis=4)), "energy", 0, 0
+            ),
+            axis=0,
+        )
+
     local_count = sigma_old.shape[0]
     size_order = sigma_old.shape[-1]
     groups = lax.axis_size("energy")
@@ -127,7 +136,7 @@
         local_count, 2, 3, 2, size_order * size_order
     )
     gathered, spectra = (
-        lax.all_to_all(outgoing, "energy", split_axis=4, concat_axis=0, tiled=True),
+        see_fields_on_mesh(outgoing),
         lax.all_to_all(kernels, "energy", split_axis=4, concat_axis=0, tiled=True),
     )
     padded_length = 2 * energies_all

time: 1390 us -> 1220 us (0.88)
  local copies, waits for them, and re-layouts: 384 us -> 218 us
    unnamed x33 -> x21, local copies, waits for them, and re-layouts: 257 us -> 142 us
    reshape x1 -> x0, local copies, waits for them, and re-layouts: 30.3 us -> none  [local(): jnp.transpose(both_kinds, (2, 0, 3, 1, 4, 5))]
    all_to_all x1 -> x0, local copies, waits for them, and re-layouts: 26.9 us -> none  [local(): lax.all_to_all(outgoing, 'energy', split_axis=4, concat_axis=0, tiled=True)]
    another operation x48 -> x52, local copies, waits for them, and re-layouts: 31.5 us -> 35.9 us
  transfers between devices with their start and end apart: 18 -> 18, of which waited for: 15 -> 15; matrix products, arithmetic and copies ran while one was open for 83% -> 89% of each run, Pallas kernels for 0% -> 0%
where the time goes in v1:
time: 1220 us
  other arithmetic  807 us (66%)
  local copies, waits for them, and re-layouts  218 us (18%)
  matrix products  71.1 us (6%)
  starting transfers between devices  68.4 us (6%)
  waiting for transfers between devices  43.8 us (4%)
    another operation x70, other arithmetic, invert(): factor = jnp.linalg.cholesky(normal)  503 us
    another operation x31, other arithmetic, invert(): lax.linalg.triangular_solve(factor, middle, left_side=True, lower=True, t...  296 us
    unnamed x21, local copies, waits for them, and re-layouts  142 us
    dot_general x132, matrix products, matmul_high(): return jnp.matmul(first, second, precision=PRECISE)  50.8 us
    ppermute x15, starting transfers between devices, passed_along(): return lax.ppermute(block, axis, route)  35.7 us
    ppermute x15, waiting for transfers between devices, passed_along(): return lax.ppermute(block, axis, route)  33.3 us
    another operation x48, local copies, waits for them, and re-layouts  32.6 us
    all_to_all x2, local copies, waits for them, and re-layouts, local(): lax.all_to_all(kernels, 'energy', split_axis=4, concat_axis=0, tiled=True)  27.3 us
  transfers between devices with their start and end apart: 18, of which 15 were waited for; matrix products, arithmetic and copies ran while one was open for 89% of the time, Pallas kernels for 0%

profile of v1, /device:TPU:1, one launch (start us, length us, event | category | flops | bytes accessed | tf_op | source)
XLA Modules:
  0.0 1215.5 jit_solution(7406681483031686523)
XLA Ops:
  3.1 24.3 %copy.289 = f32[1,1,2,3,2,128,128]{3,4,2,6,5,1,0:T(2,128)} copy(f32[1,1,2,3,2,128,128]{6,5,4,3,2,1,0:T(8,128)} %param.9) | data formatting | bytes 1572864 | tf_op args[3]
  27.4 50.3 %reshape.1293 = f32[32,1,6144]{2,1,0:T(1,128)} reshape(f32[16384,1,2,2,3]{4,3,2,1,0:T(2,128)} %bitcast.717) | data formatting | bytes 1572864
  87.5 894.8 %while.14 = (s32[]{:T(128)}, f32[2,2,1,128,128]{4,3,0,2,1:T(8,128)S(1)}, pred[]{:T(512)}, f32[2,2,1,128,128]{4,3,1,2,0:T(8,128)S(1)}, f32[2,2,1,128,128]{4,3,1,2...) while((s32[]{:T(128)}, ...), condition=%wide.region_5.6_spmd, body=%wide.region_0.5_spmd.sunk | while | flops 1009058304 | bytes 19206544 | solution.py:113
  92.5 23.5 %custom-call.47 = f32[2,1,128,128]{3,2,1,0:T(8,128)S(1)} custom-call(f32[2,1,128,128]{3,2,1,0:T(8,128)S(1)} %cholesky.395), custom_call_target="Cholesky" | custom-call | tf_op jit(solution)/shard_map/while/body/eval_jaxpr/jit(cholesky)/cholesky | solution.py:38
  136.3 23.5 %custom-call.49 = f32[2,1,128,128]{3,2,1,0:T(8,128)S(1)} custom-call(f32[2,1,128,128]{3,2,1,0:T(8,128)S(1)} %fusion.434), custom_call_target="Cholesky" | custom-call | tf_op jit(solution)/shard_map/while/body/eval_jaxpr/jit(cholesky)/cholesky | solution.py:38
  164.3 39.3 %custom-call.51 = f32[2,1,2,128,128]{3,4,2,1,0:T(8,128)S(1)} custom-call(f32[2,1,2,128,128]{4,3,2,1,0:T(8,128)S(1)} %bitcast.745), custom_call_target="InvertDiagBlocksLowerTriangular" | custom-call | tf_op jit(solution)/shard_map/while/body/eval_jaxpr/triangular_solve | solution.py:43
  221.5 23.5 %custom-call.47 = f32[2,1,128,128]{3,2,1,0:T(8,128)S(1)} custom-call(f32[2,1,128,128]{3,2,1,0:T(8,128)S(1)} %cholesky.395), custom_call_target="Cholesky" | custom-call | tf_op jit(solution)/shard_map/while/body/eval_jaxpr/jit(cholesky)/cholesky | solution.py:38
  265.4 23.5 %custom-call.49 = f32[2,1,128,128]{3,2,1,0:T(8,128)S(1)} custom-call(f32[2,1,128,128]{3,2,1,0:T(8,128)S(1)} %fusion.434), custom_call_target="Cholesky" | custom-call | tf_op jit(solution)/shard_map/while/body/eval_jaxpr/jit(cholesky)/cholesky | solution.py:38
  293.4 39.3 %custom-call.51 = f32[2,1,2,128,128]{3,4,2,1,0:T(8,128)S(1)} custom-call(f32[2,1,2,128,128]{4,3,2,1,0:T(8,128)S(1)} %bitcast.745), custom_call_target="InvertDiagBlocksLowerTriangular" | custom-call | tf_op jit(solution)/shard_map/while/body/eval_jaxpr/triangular_solve | solution.py:43
  350.3 23.5 %custom-call.47 = f32[2,1,128,128]{3,2,1,0:T(8,128)S(1)} custom-call(f32[2,1,128,128]{3,2,1,0:T(8,128)S(1)} %cholesky.395), custom_call_target="Cholesky" | custom-call | tf_op jit(solution)/shard_map/while/body/eval_jaxpr/jit(cholesky)/cholesky | solution.py:38
  394.2 23.5 %custom-call.49 = f32[2,1,128,128]{3,2,1,0:T(8,128)S(1)} custom-call(f32[2,1,128,128]{3,2,1,0:T(8,128)S(1)} %fusion.434), custom_call_target="Cholesky" | custom-call | tf_op jit(solution)/shard_map/while/body/eval_jaxpr/jit(cholesky)/cholesky | solution.py:38
  422.2 39.3 %custom-call.51 = f32[2,1,2,128,128]{3,4,2,1,0:T(8,128)S(1)} custom-call(f32[2,1,2,128,128]{4,3,2,1,0:T(8,128)S(1)} %bitcast.745), custom_call_target="InvertDiagBlocksLowerTriangular" | custom-call | tf_op jit(solution)/shard_map/while/body/eval_jaxpr/triangular_solve | solution.py:43
  478.4 23.5 %custom-call.47 = f32[2,1,128,128]{3,2,1,0:T(8,128)S(1)} custom-call(f32[2,1,128,128]{3,2,1,0:T(8,128)S(1)} %cholesky.395), custom_call_target="Cholesky" | custom-call | tf_op jit(solution)/shard_map/while/body/eval_jaxpr/jit(cholesky)/cholesky | solution.py:38
  522.2 23.5 %custom-call.49 = f32[2,1,128,128]{3,2,1,0:T(8,128)S(1)} custom-call(f32[2,1,128,128]{3,2,1,0:T(8,128)S(1)} %fusion.434), custom_call_target="Cholesky" | custom-call | tf_op jit(solution)/shard_map/while/body/eval_jaxpr/jit(cholesky)/cholesky | solution.py:38
  550.2 39.3 %custom-call.51 = f32[2,1,2,128,128]{3,4,2,1,0:T(8,128)S(1)} custom-call(f32[2,1,2,128,128]{4,3,2,1,0:T(8,128)S(1)} %bitcast.745), custom_call_target="InvertDiagBlocksLowerTriangular" | custom-call | tf_op jit(solution)/shard_map/while/body/eval_jaxpr/triangular_solve | solution.py:43
  605.7 23.5 %custom-call.47 = f32[2,1,128,128]{3,2,1,0:T(8,128)S(1)} custom-call(f32[2,1,128,128]{3,2,1,0:T(8,128)S(1)} %cholesky.395), custom_call_target="Cholesky" | custom-call | tf_op jit(solution)/shard_map/while/body/eval_jaxpr/jit(cholesky)/cholesky | solution.py:38
  649.6 23.5 %custom-call.49 = f32[2,1,128,128]{3,2,1,0:T(8,128)S(1)} custom-call(f32[2,1,128,128]{3,2,1,0:T(8,128)S(1)} %fusion.434), custom_call_target="Cholesky" | custom-call | tf_op jit(solution)/shard_map/while/body/eval_jaxpr/jit(cholesky)/cholesky | solution.py:38
  677.6 39.3 %custom-call.51 = f32[2,1,2,128,128]{3,4,2,1,0:T(8,128)S(1)} custom-call(f32[2,1,2,128,128]{4,3,2,1,0:T(8,128)S(1)} %bitcast.745), custom_call_target="InvertDiagBlocksLowerTriangular" | custom-call | tf_op jit(solution)/shard_map/while/body/eval_jaxpr/triangular_solve | solution.py:43
  733.2 23.5 %custom-call.47 = f32[2,1,128,128]{3,2,1,0:T(8,128)S(1)} custom-call(f32[2,1,128,128]{3,2,1,0:T(8,128)S(1)} %cholesky.395), custom_call_target="Cholesky" | custom-call | tf_op jit(solution)/shard_map/while/body/eval_jaxpr/jit(cholesky)/cholesky | solution.py:38
  777.0 23.5 %custom-call.49 = f32[2,1,128,128]{3,2,1,0:T(8,128)S(1)} custom-call(f32[2,1,128,128]{3,2,1,0:T(8,128)S(1)} %fusion.434), custom_call_target="Cholesky" | custom-call | tf_op jit(solution)/shard_map/while/body/eval_jaxpr/jit(cholesky)/cholesky | solution.py:38
  805.0 39.3 %custom-call.51 = f32[2,1,2,128,128]{3,4,2,1,0:T(8,128)S(1)} custom-call(f32[2,1,2,128,128]{4,3,2,1,0:T(8,128)S(1)} %bitcast.745), custom_call_target="InvertDiagBlocksLowerTriangular" | custom-call | tf_op jit(solution)/shard_map/while/body/eval_jaxpr/triangular_solve | solution.py:43
  931.6 39.3 %custom-call.51 = f32[2,1,2,128,128]{3,4,2,1,0:T(8,128)S(1)} custom-call(f32[2,1,2,128,128]{4,3,2,1,0:T(8,128)S(1)} %bitcast.745), custom_call_target="InvertDiagBlocksLowerTriangular" | custom-call | tf_op jit(solution)/shard_map/while/body/eval_jaxpr/triangular_solve | solution.py:43
  1080.3 64.8 %reshape.1294 = f32[16384,1,2,2,3]{4,3,2,1,0:T(2,128)} reshape(f32[32,6144]{1,0:T(8,128)S(1)} %reduce.40) | data formatting | bytes 1572864
  1145.0 26.8 %copy.317 = f32[1,2,3,2,32,512]{5,4,3,2,1,0:T(8,128)S(1)} copy(f32[1,2,3,2,32,512]{2,3,1,5,4,0:T(2,128)} %bitcast.716) | data formatting | bytes 1572864 | tf_op jit(solution)/shard_map/all_to_all | solution.py:140
  (538 shorter events, 518.5 us)
Async XLA Ops:
  1.6 84.7 %copy-start = (f32[1,2,128,128]{3,2,1,0:T(8,128)S(1)}, f32[1,2,128,128]{3,2,1,0:T(8,128)}, u32[]{:S(2)}) copy-start(f32[1,2,128,128]{3,2,1,0:T(8,128)} %param.7) | copy-start | bytes 393220
  1.6 84.9 %copy-start.5 = (f32[1,2,128,128]{3,2,1,0:T(8,128)S(1)}, f32[1,2,128,128]{3,2,1,0:T(8,128)}, u32[]{:S(2)}) copy-start(f32[1,2,128,128]{3,2,1,0:T(8,128)} %param.6) | copy-start | bytes 393220
  1.7 85.1 %copy-start.6 = (f32[1,1,2,128,128]{4,3,2,1,0:T(8,128)S(1)}, f32[1,1,2,128,128]{4,3,2,1,0:T(8,128)}, u32[]{:S(2)}) copy-start(f32[1,1,2,128,128]{4,3,2,1,0:T(8,128)} %param.8) | copy-start | bytes 393220
  1.7 85.6 %collective-permute-start.2 = (f32[2,128,128]{1,2,0:T(8,128)S(1)}, f32[2,128,128]{1,2,0:T(8,128)S(1)}, u32[]{:S(2)}, u32[]{:S(2)}) collective-permute-start(f32[2,128,128]{1,2,0:T(8,128)S(1)} %bitcast.744), channel_id=1, source_target_pairs={{1,0},{2,1},{3,2},{4,3},{5,4},{6,5},{7,6},{9,8},{10,9},{11,10},{12... | collective-permute-start | bytes 393224 | tf_op jit(solution)/shard_map/ppermute | solution.py:15
  77.7 981.6 %all-to-all-start.1 = ((f32[32,1,6144]{2,1,0:T(1,128)}), f32[32,1,6144]{2,1,0:T(1,128)}, u32[]{:S(2)}, u32[]{:S(2)}) async-start(f32[32,1,6144]{2,1,0:T(1,128)} %reshape.1293), calls=%async_computation.1 | async-start | bytes 1572864 | tf_op jit(solution)/shard_map/all_to_all | solution.py:140
  205.7 6.8 collective-permute-start.1
  210.0 6.7 collective-permute-start
  334.8 5.5 collective-permute-start.1
  338.3 7.2 collective-permute-start
  463.6 6.2 collective-permute-start.1
  467.9 5.7 collective-permute-start
  591.6 5.5 collective-permute-start.1
  595.2 5.8 collective-permute-start
  719.0 5.6 collective-permute-start.1
  722.7 5.7 collective-permute-start
  846.4 4.7 collective-permute-start.1
  849.2 5.7 collective-permute-start
  972.9 5.1 collective-permute-start.1
  976.1 5.7 collective-permute-start
  1051.2 4.4 copy-start.3
  1052.6 3.0 copy-start.1
  1052.9 2.7 copy-start.2
  1059.3 117.4 %all-to-all-start = ((f32[32,1,2,3,2,512]{5,4,3,2,1,0:T(2,128)}), f32[32,1,2,3,2,512]{5,4,3,2,1,0:T(2,128)S(1)}, u32[]{:S(2)}, u32[]{:S(2)}) async-start(f32[32,1,2,3,2,512]{5,4,3,2,1,0:T(2,128)} %copy.288), calls=%async_computation | async-start | bytes 1572864 | tf_op jit(solution)/shard_map/all_to_all | solution.py:67
  1192.2 21.6 %all-to-all-start.2 = ((f32[32,2,3,2,512]{4,3,2,1,0:T(2,128)}), f32[32,2,3,2,512]{4,3,2,1,0:T(2,128)S(1)}, u32[]{:S(2)}, u32[]{:S(2)}) async-start(f32[32,2,3,2,512]{4,3,2,1,0:T(2,128)} %copy.293), calls=%async_computation.2 | async-start | bytes 1572864 | tf_op jit(solution)/shard_map/all_to_all | solution.py:162
  (1 other events, 1.0 us)
